TPU v7x, 32 devices: a whole 2x2x4 slice. The times are simulated.
32 devices in a mesh: grp: 4 (over z), shard: 8 (over y, x, core).
Axes of the slice: x: 2, y: 2, z: 4, core: 2. Of those that a mesh axis runs over, the one named last changes fastest.
Arguments:
- frames_in: float32 [128, 256, 768], P(('grp', 'shard')), may hold values from -6 to 6
- cotangent: float32 [128, 256, 768], P(('grp', 'shard')), may hold values from -6 to 6
- time_table: bfloat16 [1000, 768], P(None, 'shard'), may hold values from -6 to 6
- ada_weight: bfloat16 [768, 6912], P('shard'), may hold values from -0.21875 to 0.21875
- ada_bias: bfloat16 [6912], P('shard'), may hold values from -4 to 4
- space_qkv: bfloat16 [768, 2304], P('shard'), may hold values from -0.21875 to 0.21875
- space_out: bfloat16 [768, 768], P('shard'), may hold values from -2.5 to 2.5
- time_qkv: bfloat16 [768, 2304], P('shard'), may hold values from -0.21875 to 0.21875
- time_out: bfloat16 [768, 768], P('shard'), may hold values from -0.875 to 0.875
- up_weight: bfloat16 [768, 3072], P('shard'), may hold values from -0.21875 to 0.21875
- up_bias: bfloat16 [3072], P('shard'), may hold values from -6 to 6
- down_weight: bfloat16 [3072, 768], P('shard'), may hold values from -0.109375 to 0.109375
- down_bias: bfloat16 [768], P('shard'), may hold values from -4 to 4
- timesteps: int32 [8], P('grp'), may hold values from 0 to 999
- task_mask: int32 [8, 16], P('grp'), may hold values 0 or 1
- clip_weight: float32 [8], P('grp'), may hold values from 0.5 to 2
- frame_table: int32 [4, 32], P('grp'), may hold values from 0 to 31, each once within a row
Outputs:
- frames_out: float32 [128, 256, 768], P(('grp', 'shard'))
- grad_frames_in: float32 [128, 256, 768], P(('grp', 'shard'))
- grad_time_table: float32 [1000, 768], P(None, 'shard')
- grad_ada_weight: float32 [768, 6912], P('shard')
- grad_ada_bias: float32 [6912], P('shard')
- grad_space_qkv: float32 [768, 2304], P('shard')
- grad_space_out: float32 [768, 768], P('shard')
- grad_time_qkv: float32 [768, 2304], P('shard')
- grad_time_out: float32 [768, 768], P('shard')
- grad_up_weight: float32 [768, 3072], P('shard')
- grad_up_bias: float32 [3072], P('shard')
- grad_down_weight: float32 [3072, 768], P('shard')
- grad_down_bias: float32 [768], P('shard')
Inputs may be any that keep to these rules, and one draw needn't show every extreme that they name: `frame_table`: each row lists every frame of its group once.
All inputs are finite; a program needn't handle non-finite values. No bound on the sum of `task_mask` on one device may be relied on, other than what follows from the above.
Results may differ from a plain program's by a relative error of at most 0.014.
Values may be sent and summed in bfloat16 or wider, within the bound.
No kernel may reach another device: no remote copies, remote signals or barrier semaphores. Data moves between devices by JAX's collectives and lax.ppermute only.
A program may use at most 256 MiB of HBM per device.

v0:
```python
from functools import partial
import jax
import jax.numpy as jnp
from jax import lax
from jax.sharding import PartitionSpec as P

HEADS = 12
HEAD_DIM = 64
HIGH = lax.Precision.HIGHEST
EPSILON = 1e-06


def layer_norm(values):
    center = values - jnp.mean(values, axis=-1, keepdims=True)
    spread = jnp.mean(center * center, axis=-1, keepdims=True)
    inverse = lax.rsqrt(spread + EPSILON)
    return (center * inverse, inverse)


def norm_back(grad_normed, normed, inverse):
    first = jnp.mean(grad_normed, axis=-1, keepdims=True)
    second = jnp.mean(grad_normed * normed, axis=-1, keepdims=True)
    return inverse * (grad_normed - first - normed * second)


def split_heads(packed, width):
    shape = packed.shape[:-1] + (HEADS, HEAD_DIM)
    return (
        packed[..., :width].reshape(shape),
        packed[..., width : 2 * width].reshape(shape),
        packed[..., 2 * width :].reshape(shape),
    )


def attend_forward(packed):
    width = packed.shape[-1] // 3
    query, keys, values = split_heads(packed, width)
    scores = jnp.einsum(
        "blmhe,bkmhe->bmhlk", query, keys, preferred_element_type=jnp.float32
    ) * HEAD_DIM ** (-0.5)
    highest = jnp.max(scores, axis=-1, keepdims=True)
    logsum = highest + jnp.log(jnp.sum(jnp.exp(scores - highest), axis=-1, keepdims=True))
    probs = jnp.exp(scores - logsum).astype(jnp.bfloat16)
    mixed = jnp.einsum("bmhlk,bkmhe->blmhe", probs, values, preferred_element_type=jnp.float32)
    return (mixed.reshape(packed.shape[:-1] + (width,)).astype(jnp.bfloat16), logsum)


def attend_backward(packed, logsum, grad_mixed):
    width = packed.shape[-1] // 3
    query, keys, values = split_heads(packed, width)
    factor = HEAD_DIM ** (-0.5)
    scores = (
        jnp.einsum("blmhe,bkmhe->bmhlk", query, keys, preferred_element_type=jnp.float32) * factor
    )
    probs = jnp.exp(scores - logsum)
    grad_heads = grad_mixed.reshape(query.shape)
    grad_probs = jnp.einsum(
        "blmhe,bkmhe->bmhlk", grad_heads, values, preferred_element_type=jnp.float32
    )
    grad_values = jnp.einsum(
        "bmhlk,blmhe->bkmhe",
        probs.astype(jnp.bfloat16),
        grad_heads,
        preferred_element_type=jnp.float32,
    )
    grad_scores = (
        probs * (grad_probs - jnp.sum(probs * grad_probs, axis=-1, keepdims=True))
    ).astype(jnp.bfloat16)
    grad_query = (
        jnp.einsum("bmhlk,bkmhe->blmhe", grad_scores, keys, preferred_element_type=jnp.float32)
        * factor
    )
    grad_keys = (
        jnp.einsum("bmhlk,blmhe->bkmhe", grad_scores, query, preferred_element_type=jnp.float32)
        * factor
    )
    shape = packed.shape[:-1] + (width,)
    joined = jnp.concatenate(
        [grad_query.reshape(shape), grad_keys.reshape(shape), grad_values.reshape(shape)], axis=-1
    )
    return joined.astype(jnp.bfloat16)


def mixer_forward(resid, shift, scale, gate, qkv_weight, out_weight):
    normed, inverse = layer_norm(resid)
    entry = (normed * (1.0 + scale) + shift).astype(jnp.bfloat16)
    packed = jnp.einsum(
        "blmd,de->blme", entry, qkv_weight, preferred_element_type=jnp.float32
    ).astype(jnp.bfloat16)
    mixed, logsum = attend_forward(packed)
    branch = jnp.einsum("blmd,de->blme", mixed, out_weight, preferred_element_type=jnp.float32)
    return (resid + gate * branch, (normed, inverse, entry, packed, logsum, mixed, branch))


def mixer_backward(grad_out, scale, gate, qkv_weight, out_weight, kept, per_clip):
    normed, inverse, entry, packed, logsum, mixed, branch = kept
    grad_gate = per_clip(grad_out * branch)
    grad_branch = (gate * grad_out).astype(jnp.bfloat16)
    grad_outw = jnp.einsum("blmd,blme->de", mixed, grad_branch, preferred_element_type=jnp.float32)
    grad_mixed = jnp.einsum(
        "blme,de->blmd", grad_branch, out_weight, preferred_element_type=jnp.float32
    ).astype(jnp.bfloat16)
    grad_packed = attend_backward(packed, logsum, grad_mixed)
    grad_qkvw = jnp.einsum("blmd,blme->de", entry, grad_packed, preferred_element_type=jnp.float32)
    grad_entry = jnp.einsum(
        "blme,de->blmd", grad_packed, qkv_weight, preferred_element_type=jnp.float32
    )
    grad_shift = per_clip(grad_entry)
    grad_scale = per_clip(grad_entry * normed)
    grad_in = grad_out + norm_back(grad_entry * (1.0 + scale), normed, inverse)
    return (grad_in, (grad_shift, grad_scale, grad_gate), grad_qkvw, grad_outw)


def feed_forward(resid, shift, scale, gate, up_full, up_bias_full, down_full, down_bias_full):
    normed, inverse = layer_norm(resid)
    entry = (normed * (1.0 + scale) + shift).astype(jnp.bfloat16)
    upward = jnp.einsum(
        "blmd,df->blmf", entry, up_full, preferred_element_type=jnp.float32
    ) + up_bias_full.astype(jnp.float32)
    active = jax.nn.gelu(upward, approximate=False).astype(jnp.bfloat16)
    downward = jnp.einsum(
        "blmf,fd->blmd", active, down_full, preferred_element_type=jnp.float32
    ) + down_bias_full.astype(jnp.float32)
    return (resid + gate * downward, (normed, inverse, entry, upward, active, downward))


def feed_backward(grad_out, scale, gate, up_full, down_full, kept, per_clip):
    normed, inverse, entry, upward, active, downward = kept
    grad_gate = per_clip(grad_out * downward)
    grad_down_in = (gate * grad_out).astype(jnp.bfloat16)
    grad_down = jnp.einsum(
        "blmf,blmd->fd", active, grad_down_in, preferred_element_type=jnp.float32
    )
    grad_down_bias = jnp.sum(grad_down_in.astype(jnp.float32), axis=(0, 1, 2))
    grad_active = jnp.einsum(
        "blmd,fd->blmf", grad_down_in, down_full, preferred_element_type=jnp.float32
    )
    _, gelu_back = jax.vjp(partial(jax.nn.gelu, approximate=False), upward)
    grad_up_in = gelu_back(grad_active)[0].astype(jnp.bfloat16)
    grad_up = jnp.einsum("blmd,blmf->df", entry, grad_up_in, preferred_element_type=jnp.float32)
    grad_up_bias = jnp.sum(grad_up_in.astype(jnp.float32), axis=(0, 1, 2))
    grad_entry = jnp.einsum(
        "blmf,df->blmd", grad_up_in, up_full, preferred_element_type=jnp.float32
    )
    grad_shift = per_clip(grad_entry)
    grad_scale = per_clip(grad_entry * normed)
    grad_in = grad_out + norm_back(grad_entry * (1.0 + scale), normed, inverse)
    return (
        grad_in,
        (grad_shift, grad_scale, grad_gate),
        grad_up,
        grad_up_bias,
        grad_down,
        grad_down_bias,
    )


def body(
    frames_in,
    cotangent,
    time_table,
    ada_weight,
    ada_bias,
    space_qkv,
    space_out,
    time_qkv,
    time_out,
    up_weight,
    up_bias,
    down_weight,
    down_bias,
    timesteps,
    task_mask,
    clip_weight,
    frame_table,
):
    shards = lax.axis_size("shard")
    shard_at = lax.axis_index("shard")
    frame_count, patches, width = frames_in.shape
    clips = timesteps.shape[0]
    frames = task_mask.shape[1]
    table = frame_table[0]
    group_frames = table.shape[0]
    columns = patches // shards
    space_qkv_full = lax.all_gather(space_qkv, "shard", axis=0, tiled=True)
    space_out_full = lax.all_gather(space_out, "shard", axis=0, tiled=True)
    time_qkv_full = lax.all_gather(time_qkv, "shard", axis=0, tiled=True)
    time_out_full = lax.all_gather(time_out, "shard", axis=0, tiled=True)
    up_full = lax.all_gather(up_weight, "shard", axis=0, tiled=True)
    down_full = lax.all_gather(down_weight, "shard", axis=0, tiled=True)
    embed = jnp.take(time_table, timesteps, axis=0).astype(jnp.float32)
    cond = jax.nn.silu(embed).astype(jnp.bfloat16)
    mod_local = jnp.dot(cond, ada_weight, preferred_element_type=jnp.float32)

    def spread(local):
        full = jnp.zeros((shards, local.shape[0]), jnp.float32)
        return lax.dynamic_update_slice_in_dim(
            full, local.astype(jnp.float32)[None], shard_at, 0
        ).reshape(-1)

    small = jnp.concatenate(
        [(mod_local + spread(ada_bias)[None]).reshape(-1), spread(up_bias), spread(down_bias)]
    )
    small = lax.psum(small, "shard")
    modul = small[: clips * 9 * width].reshape(clips, 9 * width)
    up_bias_full = small[clips * 9 * width : -width]
    down_bias_full = small[-width:]
    slot_ids = shard_at * frame_count + jnp.arange(frame_count, dtype=jnp.int32)
    frame_ids = jnp.take(table, slot_ids)
    clip_of = frame_ids // frames
    frame_of = frame_ids % frames
    clip_hot = (clip_of[:, None] == jnp.arange(clips, dtype=jnp.int32)[None, :]).astype(jnp.float32)
    frame_mod = jnp.take(modul, clip_of, axis=0)
    own_parts = [
        frame_mod[:, part_at * width : (part_at + 1) * width][:, None, None, :]
        for part_at in range(9)
    ]
    all_parts = [
        modul[:, part_at * width : (part_at + 1) * width][:, None, None, :] for part_at in range(9)
    ]
    inverse = (
        jnp.zeros((group_frames,), jnp.int32)
        .at[table]
        .set(jnp.arange(group_frames, dtype=jnp.int32))
    )

    def frame_sums(values):
        return jnp.dot(clip_hot.T, jnp.sum(values, axis=(1, 2)), precision=HIGH)

    def column_sums(values):
        return jnp.sum(values, axis=(1, 2))

    def to_columns(rows):
        parts = rows.astype(jnp.bfloat16).reshape(frame_count, shards, columns, width)
        parts = jnp.swapaxes(parts, 0, 1)
        moved = lax.all_to_all(parts, "shard", split_axis=0, concat_axis=0, tiled=True)
        return moved.reshape(group_frames, columns, width)

    def to_frames(cols):
        parts = cols.astype(jnp.bfloat16).reshape(shards, frame_count, columns, width)
        moved = lax.all_to_all(parts, "shard", split_axis=0, concat_axis=0, tiled=True)
        moved = jnp.swapaxes(moved, 0, 1)
        return moved.reshape(frame_count, patches, width).astype(jnp.float32)

    space_rows = frames_in.reshape(frame_count, patches, 1, width)
    after_space, space_kept = mixer_forward(
        space_rows, own_parts[0], own_parts[1], own_parts[2], space_qkv_full, space_out_full
    )
    received = to_columns(after_space.reshape(frame_count, patches, width))
    columned = jnp.take(received, inverse, axis=0).reshape(clips, frames, columns, width)
    columned = columned.astype(jnp.float32)
    after_time, time_kept = mixer_forward(
        columned, all_parts[3], all_parts[4], all_parts[5], time_qkv_full, time_out_full
    )
    result, mlp_kept = feed_forward(
        after_time,
        all_parts[6],
        all_parts[7],
        all_parts[8],
        up_full,
        up_bias_full,
        down_full,
        down_bias_full,
    )
    leaving = jnp.take(result.reshape(group_frames, columns, width), table, axis=0)
    frames_out = to_frames(leaving)
    row_weights = task_mask[clip_of, frame_of].astype(jnp.float32) * clip_weight[clip_of]
    weighted = cotangent * row_weights[:, None, None]
    arriving = to_columns(weighted)
    grad_result = jnp.take(arriving, inverse, axis=0).reshape(clips, frames, columns, width)
    grad_result = grad_result.astype(jnp.float32)
    grad_after_time, mlp_mods, grad_up, grad_up_bias, grad_down, grad_down_bias = feed_backward(
        grad_result, all_parts[7], all_parts[8], up_full, down_full, mlp_kept, column_sums
    )
    grad_columned, time_mods, grad_time_qkv, grad_time_out = mixer_backward(
        grad_after_time,
        all_parts[4],
        all_parts[5],
        time_qkv_full,
        time_out_full,
        time_kept,
        column_sums,
    )
    going = jnp.take(grad_columned.reshape(group_frames, columns, width), table, axis=0)
    grad_space = to_frames(going)
    grad_rows, space_mods, grad_space_qkv, grad_space_out = mixer_backward(
        grad_space.reshape(frame_count, patches, 1, width),
        own_parts[1],
        own_parts[2],
        space_qkv_full,
        space_out_full,
        space_kept,
        frame_sums,
    )
    mod_part = jnp.concatenate(space_mods + time_mods + mlp_mods, axis=1)
    small_grads = jnp.concatenate([mod_part.reshape(-1), grad_up_bias, grad_down_bias])
    small_grads = lax.psum(small_grads, "shard")
    mod_size = clips * 9 * width
    grad_modul = small_grads[:mod_size].reshape(clips, 9 * width).astype(jnp.bfloat16)
    up_dev = up_bias.shape[0]
    down_dev = down_bias.shape[0]
    bias_dev = ada_bias.shape[0]
    every_modul = lax.all_gather(grad_modul, "grp", axis=0, tiled=True)
    bias_sums = lax.psum(
        jnp.concatenate(
            [
                lax.dynamic_slice_in_dim(small_grads, mod_size + shard_at * up_dev, up_dev, 0),
                lax.dynamic_slice_in_dim(
                    small_grads, mod_size + shards * up_dev + shard_at * down_dev, down_dev, 0
                ),
            ]
        ),
        "grp",
    )
    every_embed = lax.all_gather(embed.astype(jnp.bfloat16), "grp", axis=0, tiled=True)
    every_embed = every_embed.astype(jnp.float32)
    groups = lax.axis_size("grp")
    step_slots = jnp.zeros((groups, clips), jnp.float32)
    step_slots = lax.dynamic_update_slice_in_dim(
        step_slots, timesteps.astype(jnp.float32)[None], lax.axis_index("grp"), 0
    )
    every_steps = lax.psum(step_slots.reshape(-1), "grp").astype(jnp.int32)
    every_cond = jax.nn.silu(every_embed).astype(jnp.bfloat16)
    grad_ada = jnp.einsum("cd,cj->dj", every_cond, every_modul, preferred_element_type=jnp.float32)
    grad_ada_bias = lax.dynamic_slice_in_dim(
        jnp.sum(every_modul.astype(jnp.float32), axis=0), shard_at * bias_dev, bias_dev, 0
    )
    grad_cond = jnp.einsum("cj,dj->cd", every_modul, ada_weight, preferred_element_type=jnp.float32)
    _, silu_back = jax.vjp(jax.nn.silu, every_embed)
    grad_embed = silu_back(grad_cond)[0]
    vocab = time_table.shape[0]
    onehot = (jnp.arange(vocab, dtype=jnp.int32)[:, None] == every_steps[None, :]).astype(
        jnp.float32
    )
    grad_table = jnp.dot(onehot, grad_embed, precision=HIGH)

    def total(parts):
        flat = [part.astype(jnp.bfloat16).reshape(shards, -1, width) for part in parts]
        rows = [part.shape[1] for part in flat]
        packed = jnp.concatenate(flat, axis=1)
        share = lax.psum_scatter(packed, "shard", scatter_dimension=0, tiled=True)[0]
        share = lax.psum(share, "grp").astype(jnp.float32)
        out, at = ([], 0)
        for part, count in zip(parts, rows):
            piece = share[at : at + count].reshape(part.shape[0] // shards, part.shape[1])
            out.append(piece)
            at += count
        return out

    grad_up, grad_down = total([grad_up, grad_down])
    grad_time_qkv, grad_time_out = total([grad_time_qkv, grad_time_out])
    grad_space_qkv, grad_space_out = total([grad_space_qkv, grad_space_out])
    return (
        frames_out,
        grad_rows.reshape(frame_count, patches, width),
        grad_table,
        grad_ada,
        grad_ada_bias,
        grad_space_qkv,
        grad_space_out,
        grad_time_qkv,
        grad_time_out,
        grad_up,
        bias_sums[:up_dev],
        grad_down,
        bias_sums[up_dev:],
    )


def solution(mesh):
    placed = (
        P(("grp", "shard"), None, None),
        P(("grp", "shard"), None, None),
        P(None, "shard"),
        P("shard", None),
        P("shard"),
        P("shard", None),
        P("shard", None),
        P("shard", None),
        P("shard", None),
        P("shard", None),
        P("shard"),
        P("shard", None),
        P("shard"),
        P("grp"),
        P("grp", None),
        P("grp"),
        P("grp", None),
    )
    return jax.shard_map(
        body,
        mesh=mesh,
        in_specs=placed,
        out_specs=(
            P(("grp", "shard"), None, None),
            P(("grp", "shard"), None, None),
            P(None, "shard"),
            P("shard", None),
            P("shard"),
            P("shard", None),
            P("shard", None),
            P("shard", None),
            P("shard", None),
            P("shard", None),
            P("shard"),
            P("shard", None),
            P("shard"),
        ),
        check_vma=False,
    )
```

profile of v0, /device:TPU:0, one launch (start us, length us, event | category | flops | bytes accessed | tf_op | source)
XLA Modules:
  0.0 886.2 jit_solution(1337077079453278443)
XLA Ops:
  24.4 5.2 all-to-all-start.2
  34.7 35.1 %all-reduce.6.cloned.1.call-done = f32[17664]{0:T(1024)} async-done(((f32[17664]{0:T(1024)}), f32[17664]{0:T(1024)}) %all-reduce.6.cloned.1.call-update) | async-done | bytes 70672 | tf_op jit(solution)/shard_map/psum | solution.py:204
  71.3 35.3 %all-gather.9.cloned.1.call-done = bf16[768,2304]{1,0:T(8,128)(2,1)} async-done(((bf16[96,2304]{1,0:T(8,128)(2,1)}), bf16[768,2304]{1,0:T(8,128)(2,1)}) %all-gather.9.cloned.1.call-update) | async-done | bytes 3538960 | tf_op jit(solution)/shard_map/all_gather | solution.py:185
  106.7 7.0 fusion.9
  129.4 8.7 convolution_convert_fusion.3
  138.1 5.9 add_convert_fusion.3
  156.2 23.0 %all-to-all-done = bf16[8,4,32,768]{3,2,1,0:T(8,128)(2,1)S(1)} async-done(((bf16[8,4,32,768]{3,2,1,0:T(8,128)(2,1)}), bf16[8,4,32,768]{3,2,1,0:T(8,128)(2,1)S(1)}, u32[]{:S(2)}, u32[]{:S(2)}) %all-to-all-start) | async-done | bytes 1572896 | tf_op jit(solution)/shard_map/all_to_all | solution.py:236
  182.4 5.2 select_convert_fusion.2
  189.8 7.0 convolution_convert_fusion
  199.2 6.1 reshape.639
  205.3 5.9 reshape.640
  211.1 5.9 reshape.638
  217.0 8.0 multiply_reduce_fusion.3
  238.4 6.5 convert_element_type.258
  244.9 5.8 multiply_add_fusion.3
  255.4 11.7 %fusion.8 = (u16[2,32,3072]{2,1,0:T(8,128)(2,1)S(1)}, u16[2,32,3072]{2,1,0:T(8,128)(2,1)S(1)}, f32[2,16,32,3072]{3,2,1,0:T(8,128)S(1)}) fusion(f32[3072]{0:T(1024)S(1)} %slice.149, bf16[768,3072]{1,0:T(8,128)(2,1)} %all-gather.17.cloned.1.call-done, f32[2,16,32,768]{3,2,1,0:T(8,128)} %get-tuple-element.73, f32[2,768]{1,0:T(2,128)S(1)} %get-tuple-element.54, ...), kind=kOutput, calls=%fused_computation.51 | convolution fusion | flops 4879417344 | bytes 21266432 | tf_op jit(solution)/shard_map/blmd,df->blmf/dot_general | solution.py:117
  272.0 29.8 %multiply_convert_fusion.1 = (bf16[2,16,32,3072]{3,2,1,0:T(8,128)(2,1)}, f32[2,16,32,3072]{3,2,1,0:T(8,128)}) fusion(f32[2,16,32,3072]{3,2,1,0:T(8,128)S(1)} %get-tuple-element.75, f32[3072]{0:T(1024)S(1)} %slice.149, u16[2,32,3072]{2,1,0:T(8,128)(2,1)S(1)} %get-tuple-element.16, u16[2,32,3072]{2,1,0:T(8,128)(2,1)S(1)} %get-tuple-element.15), kind=kLoop, calls=%fused_computation.21 | loop fusion | flops 223346688 | bytes 32256000 | tf_op jit(solution)/shard_map/convert_element_type | solution.py:120
  301.7 19.7 %convert_reduce_fusion = (f32[3072]{0:T(1024)}, bf16[2,16,32,3072]{3,2,1,0:T(8,128)(2,1)}) fusion(f32[2,16,32,3072]{3,2,1,0:T(8,128)} %get-tuple-element.37, bf16[3072,768]{1,0:T(8,128)(2,1)} %all-gather.19.cloned.1.call-done, f32[2,16,32,768]{3,2,1,0:T(8,128)} %bitcast.240, f32[2,768]{1,0:T(2,128)S(1)} %get-tuple-element.55, ...), kind=kOutput, calls=%fused_computation.17 | convolution fusion | flops 4886885376 | bytes 39352320 | tf_op jit(solution)/shard_map/blmd,fd->blmf/dot_general | solution.py:135
  321.4 10.0 %multiply_reduce_fusion.5 = (f32[2,768]{1,0:T(2,128)}, f32[2,16,32]{2,1,0:T(8,128)S(1)}, f32[2,16,32]{2,1,0:T(8,128)S(1)}, f32[2,768]{1,0:T(2,128)}, f32[2,16,32,768]{3,2,1,0:T(8,128)S(1)}) fusion(f32[2,16,32,768]{3,2,1,0:T(8,128)S(1)} %copy-done.10, f32[2,16,32]{2,1,0:T(8,128)S(1)} %add_rsqrt_fusion, f32[2,16,32]{2,1,0:T(8,128)S(1)} %broadcast_multiply_fusion.4, ...), kind=kOutput, calls=%fused_computation.88 | convolution fusion | flops 4838910976 | bytes 17336320 | tf_op jit(solution)/shard_map/blmf,df->blmd/dot_general | solution.py:142
  338.0 6.2 reshape.645
  344.2 13.1 %multiply_reduce_fusion.2 = (f32[2,32,12,16]{3,2,1,0:T(8,128)S(1)}, f32[2,32,12,16,16]{3,4,2,1,0:T(8,128)}) fusion(f32[2,32,12,16,16]{3,4,2,1,0:T(8,128)} %copy-done.5, f32[2,32,12,16]{3,2,1,0:T(8,128)} %copy-done.28, bf16[2,16,32,12,64]{4,3,2,1,0:T(8,128)(2,1)} %reshape.638, bf16[2,16,32,12,64]{4,3,2,1,0:T(8,128)(2,1)} %reshape.645), kind=kOutput, calls=%fused_computation.47 | convolution fusion | flops 25939968 | bytes 4816896 | tf_op jit(solution)/shard_map/blmhe,bkmhe->bmhlk/dot_general | solution.py:57
  357.3 6.7 convert_bitcast_fusion.1
  376.4 5.2 reshape.646
  386.6 6.1 reshape.647
  397.8 6.1 reshape.648
  408.1 5.8 bitcast_convert_fusion.2
  413.9 6.8 reshape.657
  425.4 10.9 %multiply_reduce_fusion.7 = (f32[2,768]{1,0:T(2,128)}, f32[2,16,32]{2,1,0:T(8,128)S(1)}, f32[2,16,32]{2,1,0:T(8,128)S(1)}, f32[2,768]{1,0:T(2,128)}, f32[2,16,32,768]{3,2,1,0:T(8,128)}) fusion(f32[2,16,32,768]{3,2,1,0:T(8,128)} %bitcast.258, f32[2,16,32]{2,1,0:T(8,128)S(1)} %bitcast.274, f32[2,16,32]{2,1,0:T(8,128)S(1)} %bitcast.270, ...), kind=kOutput, calls=%fused_computation.90 | convolution fusion | flops 3630951424 | bytes 14583808 | tf_op jit(solution)/shard_map/blme,de->blmd/dot_general | solution.py:105
  436.3 9.3 %multiply_add_fusion.2 = (bf16[2,16,32,768]{3,2,1,0:T(8,128)(2,1)}, f32[2,16,32,768]{3,2,1,0:T(8,128)}) fusion(f32[2,16,32,768]{3,2,1,0:T(8,128)S(1)} %copy-done.11, f32[768]{0:T(1024)S(1)} %copy-done.61, f32[2,768]{1,0:T(2,128)S(1)} %get-tuple-element.55, bf16[2,16,32,3072]{3,2,1,0:T(8,128)(2,1)S(1)} %bitcast.250, ...), kind=kOutput, calls=%fused_computation.103 | convolution fusion | flops 4834983936 | bytes 18883584 | tf_op jit(solution)/shard_map/blmf,fd->blmd/dot_general | solution.py:121
  465.0 10.6 %bitcast_convert_fusion.1 = bf16[768,3072]{1,0:T(8,128)(2,1)} fusion(bf16[2,16,32,3072]{3,2,1,0:T(8,128)(2,1)} %get-tuple-element.86, f32[2,16,32,768]{3,2,1,0:T(8,128)} %get-tuple-element.73, f32[2,768]{1,0:T(2,128)S(1)} %copy-done.66, f32[2,768]{1,0:T(2,128)S(1)} %get-tuple-element.53, f32[2,16,32]{2,1,0:T(8,128)S(1)} %add_rsqrt_fusion, ...), kind=kOutput, calls=%fused_computation.39 | convolution fusion | flops 4838129664 | bytes 14176256 | tf_op jit(solution)/shard_map/blmd,blmf->df/dot_general | solution.py:140
  475.6 8.5 reshape.660
  484.1 8.0 all-to-all-done.3
  502.9 8.1 convolution_convert_fusion.2
  513.7 6.9 multiply_reduce_fusion
  520.6 7.6 multiply_convert_fusion
  534.1 6.0 multiply_convert_fusion.6
  542.8 8.8 bitcast_convert_fusion.3
  551.7 6.7 reshape.654
  563.9 8.2 bitcast_convert_fusion
  572.1 6.9 pad_maximum_fusion
  591.2 7.0 multiply_reduce_fusion.8
  602.7 29.1 %reduce-scatter.4.cloned.1.call-done = bf16[1,384,768]{2,1,0:T(8,128)(2,1)} async-done(((bf16[8,384,768]{2,1,0:T(8,128)(2,1)}), bf16[1,384,768]{2,1,0:T(8,128)(2,1)}) %reduce-scatter.4.cloned.1.call-update) | async-done | bytes 589840 | tf_op jit(solution)/shard_map/reduce_scatter | solution.py:341
  631.8 80.2 %reduce-scatter.8.cloned.1.call-done = bf16[1,768,768]{2,1,0:T(8,128)(2,1)} async-done(((bf16[8,768,768]{2,1,0:T(8,128)(2,1)}), bf16[1,768,768]{2,1,0:T(8,128)(2,1)}) %reduce-scatter.8.cloned.1.call-update) | async-done | bytes 1179664 | tf_op jit(solution)/shard_map/reduce_scatter | solution.py:341
  712.2 10.9 %all-gather.1 = bf16[4,2,96]{2,1,0:T(2,128)(2,1)S(1)} all-gather(bf16[1,2,96]{2,1,0:T(2,128)(2,1)S(1)} %fusion.91), channel_id=1, replica_groups=mesh['grp'=4,'shard'=8] {'grp'}, dimensions={0}, use_global_device_ids=true | all-gather | bytes 1920 | tf_op jit(solution)/shard_map/all_gather | solution.py:315
  723.1 42.7 %all-reduce.8.cloned.1.call-done = f32[17664]{0:T(1024)} async-done(((f32[17664]{0:T(1024)}), f32[17664]{0:T(1024)}) %all-reduce.8.cloned.1.call-update) | async-done | bytes 70672 | tf_op jit(solution)/shard_map/psum | solution.py:297
  769.4 12.1 %all-reduce = (f32[8]{0:T(128)S(1)}, f32[480]{0:T(512)S(1)}) all-reduce(f32[8]{0:T(128)S(1)} %reshape.652, f32[480]{0:T(512)S(1)} %pad_maximum_fusion.8), channel_id=1, replica_groups=mesh['grp'=4,'shard'=8] {'grp'}, use_global_device_ids=true, to_apply=%region_20.23 | all-reduce | flops 488 | bytes 3904 | tf_op jit(solution)/shard_map/psum | solution.py:322
  782.9 14.5 %all-gather = bf16[4,2,6912]{2,1,0:T(2,128)(2,1)S(1)} all-gather(bf16[1,2,6912]{2,1,0:T(2,128)(2,1)S(1)} %reshape.753), channel_id=1, replica_groups=mesh['grp'=4,'shard'=8] {'grp'}, dimensions={0}, use_global_device_ids=true | all-gather | bytes 138240 | tf_op jit(solution)/shard_map/all_gather | solution.py:303
  801.9 64.0 %all-reduce.10.cloned.1.call-done = (bf16[384,768]{1,0:T(8,128)(2,1)}, bf16[384,768]{1,0:T(8,128)(2,1)}, bf16[768,768]{1,0:T(8,128)(2,1)}) async-done(((bf16[384,768]{1,0:T(8,128)(2,1)}, bf16[384,768]{1,0:T(8,128)(2,1)}, bf16[768,768]{1,0:T(8,128)(2,1)}), (bf16[384,768]{1,0:T(8,128)(2,1)}, bf16[384,768]{1,0:T(8,128)(2,1)}, bf16[768,768]{1,0:T(8,128)(2,1)})) %all-reduce.10.cloned.1.call-update) | async-done | bytes 2359312 | tf_op jit(solution)/shard_map/psum | solution.py:342
  (354 shorter events, 205.7 us)
Async XLA Ops:
  7.2 7.4 copy-start
  7.2 11.8 %copy-start.2 = (s32[1,32]{1,0:T(1,128)S(1)}, s32[1,32]{1,0:T(1,128)}, u32[]{:S(2)}) copy-start(s32[1,32]{1,0:T(1,128)} %param.37) | copy-start | bytes 388
  7.2 12.4 %copy-start.4 = (s32[2,16]{1,0:T(2,128)S(1)}, s32[2,16]{1,0:T(2,128)}, u32[]{:S(2)}) copy-start(s32[2,16]{1,0:T(2,128)} %param.35) | copy-start | bytes 388
  7.2 13.1 %copy-start.1 = (f32[2]{0:T(128)S(1)}, f32[2]{0:T(128)}, u32[]{:S(2)}) copy-start(f32[2]{0:T(128)} %param.36) | copy-start | bytes 28
  7.2 62.5 %all-reduce.6.cloned.1.call-start = ((), (), s32[]{:S(2)}) async-start(), calls=%async_computation.7 | async-start | bytes 147456 | tf_op jit(solution)/shard_map/psum | solution.py:204
  8.0 15.1 %copy-start.73 = (pred[2]{0:T(512)(128)(4,1)}, pred[2]{0:T(512)(128)(4,1)S(1)}, u32[]{:S(2)}) copy-start(pred[2]{0:T(512)(128)(4,1)S(1)} %compare_and_fusion.2) | copy-start | bytes 10
  14.6 8.6 copy-start.71
  15.7 91.0 %all-gather.9.cloned.1.call-start = ((), (), s32[]{:S(2)}) async-start(), calls=%async_computation.8 | async-start | bytes 3981312 | tf_op jit(solution)/shard_map/all_gather | solution.py:185
  16.5 121.6 %all-gather.11.cloned.1.call-start = ((), (), s32[]{:S(2)}) async-start(), calls=%async_computation.9 | async-start | bytes 1327104 | tf_op jit(solution)/shard_map/all_gather | solution.py:186
  17.2 172.6 %all-gather.13.cloned.1.call-start = ((), (), s32[]{:S(2)}) async-start(), calls=%async_computation.10 | async-start | bytes 3981312 | tf_op jit(solution)/shard_map/all_gather | solution.py:187
  17.8 227.1 %all-gather.15.cloned.1.call-start = ((), (), s32[]{:S(2)}) async-start(), calls=%async_computation.11 | async-start | bytes 1327104 | tf_op jit(solution)/shard_map/all_gather | solution.py:188
  18.4 237.0 %all-gather.17.cloned.1.call-start = ((), (), s32[]{:S(2)}) async-start(), calls=%async_computation.12 | async-start | bytes 5308416 | tf_op jit(solution)/shard_map/all_gather | solution.py:189
  24.4 120.8 %all-to-all-start.2 = ((bf16[8,4,32,768]{3,2,1,0:T(8,128)(2,1)}), bf16[8,4,32,768]{3,2,1,0:T(8,128)(2,1)}, u32[]{:S(2)}, u32[]{:S(2)}) async-start(bf16[8,4,32,768]{3,2,1,0:T(8,128)(2,1)} %copy.168), calls=%async_computation.2 | async-start | bytes 3145728 | tf_op jit(solution)/shard_map/all_to_all | solution.py:236
  32.3 81.4 %copy-start.56 = (f32[4,256]{1,0:T(4,128)}, f32[4,256]{1,0:T(4,128)S(1)}, u32[]{:S(2)}) copy-start(f32[4,256]{1,0:T(4,128)S(1)} %broadcast_multiply_fusion.8) | copy-start | bytes 12292
  34.7 79.1 %copy-start.59 = (f32[4,256]{1,0:T(4,128)}, f32[4,256]{1,0:T(4,128)S(1)}, u32[]{:S(2)}) copy-start(f32[4,256]{1,0:T(4,128)S(1)} %add_rsqrt_fusion.2) | copy-start | bytes 12292
  71.3 42.4 %copy-start.54 = (f32[4,768]{1,0:T(4,128)}, f32[4,768]{1,0:T(4,128)S(1)}, u32[]{:S(2)}) copy-start(f32[4,768]{1,0:T(4,128)S(1)} %get-tuple-element.52) | copy-start | bytes 36868
  71.3 42.4 %copy-start.62 = (f32[4,768]{1,0:T(4,128)}, f32[4,768]{1,0:T(4,128)S(1)}, u32[]{:S(2)}) copy-start(f32[4,768]{1,0:T(4,128)S(1)} %get-tuple-element.51) | copy-start | bytes 36868
  71.3 66.7 %copy-start.52 = (f32[4,768]{1,0:T(4,128)}, f32[4,768]{1,0:T(4,128)S(1)}, u32[]{:S(2)}) copy-start(f32[4,768]{1,0:T(4,128)S(1)} %get-tuple-element.50) | copy-start | bytes 36868
  127.4 10.6 %copy-start.43 = (f32[4,12,256]{2,1,0:T(8,128)}, f32[4,12,256]{2,1,0:T(8,128)S(1)}, u32[]{:S(2)}) copy-start(f32[4,12,256]{2,1,0:T(8,128)S(1)} %log_add_fusion.1) | copy-start | bytes 147460
  129.4 8.7 copy-start.25
  145.2 34.0 %all-to-all-start = ((bf16[8,4,32,768]{3,2,1,0:T(8,128)(2,1)}), bf16[8,4,32,768]{3,2,1,0:T(8,128)(2,1)S(1)}, u32[]{:S(2)}, u32[]{:S(2)}) async-start(bf16[8,4,32,768]{3,2,1,0:T(8,128)(2,1)} %bitcast.226), calls=%async_computation | async-start | bytes 3145728 | tf_op jit(solution)/shard_map/all_to_all | solution.py:236
  148.8 153.0 %all-gather.19.cloned.1.call-start = ((), (), s32[]{:S(2)}) async-start(), calls=%async_computation.13 | async-start | bytes 5308416 | tf_op jit(solution)/shard_map/all_gather | solution.py:190
  149.5 453.2 %reduce-scatter.6.cloned.1.call-start = ((), (), s32[]{:S(2)}) async-start(), calls=%async_computation.16 | async-start | bytes 5308416 | tf_op jit(solution)/shard_map/reduce_scatter | solution.py:341
  152.9 102.4 %copy-start.65 = (f32[2,768]{1,0:T(2,128)}, f32[2,768]{1,0:T(2,128)S(1)}, u32[]{:S(2)}) copy-start(f32[2,768]{1,0:T(2,128)S(1)} %get-tuple-element.54) | copy-start | bytes 18436
  182.4 62.6 %copy-start.6 = (bf16[32,32,768]{2,1,0:T(8,128)(2,1)}, bf16[32,32,768]{2,1,0:T(8,128)(2,1)S(1)}, u32[]{:S(2)}) copy-start(bf16[32,32,768]{2,1,0:T(8,128)(2,1)S(1)} %gather_fusion.5) | copy-start | bytes 4718596
  301.7 19.7 %copy-start.10 = (f32[2,16,32,768]{3,2,1,0:T(8,128)S(1)}, f32[2,16,32,768]{3,2,1,0:T(8,128)}, u32[]{:S(2)}) copy-start(f32[2,16,32,768]{3,2,1,0:T(8,128)} %get-tuple-element.73) | copy-start | bytes 9437188
  321.4 10.0 %copy-start.20 = (bf16[32,32,768]{2,1,0:T(8,128)(2,1)S(1)}, bf16[32,32,768]{2,1,0:T(8,128)(2,1)}, u32[]{:S(2)}) copy-start(bf16[32,32,768]{2,1,0:T(8,128)(2,1)} %gather_fusion.7) | copy-start | bytes 4718596
  338.0 19.4 %slice-start = ((s8[6291456]{0:T(1024)(128)(4,1)}), s8[2097152]{0:T(1024)(128)(4,1)S(1)}, s32[]{:S(2)}) async-start(s8[6291456]{0:T(1024)(128)(4,1)} %bitcast.230), calls=%async_computation.19 | async-start | bytes 4194304
  344.2 13.1 %slice-start.1 = ((s8[6291456]{0:T(1024)(128)(4,1)}), s8[4194304]{0:T(1024)(128)(4,1)S(1)}, s32[]{:S(2)}) async-start(s8[6291456]{0:T(1024)(128)(4,1)} %bitcast.230), calls=%async_computation.20 | async-start | bytes 8388608
  344.2 13.1 %copy-start.29 = (f32[2,32,12,16]{3,2,1,0:T(8,128)S(1)}, f32[2,32,12,16]{3,2,1,0:T(8,128)}, u32[]{:S(2)}) copy-start(f32[2,32,12,16]{3,2,1,0:T(8,128)} %copy-done.28) | copy-start | bytes 147460
  425.3 11.0 %slice-start.2 = ((s8[6291456]{0:T(1024)(128)(4,1)}), s8[2097152]{0:T(1024)(128)(4,1)S(1)}, s32[]{:S(2)}) async-start(s8[6291456]{0:T(1024)(128)(4,1)} %bitcast.249), calls=%async_computation.21 | async-start | bytes 4194304
  425.3 11.0 %copy-start.11 = (f32[2,16,32,768]{3,2,1,0:T(8,128)S(1)}, f32[2,16,32,768]{3,2,1,0:T(8,128)}, u32[]{:S(2)}) copy-start(f32[2,16,32,768]{3,2,1,0:T(8,128)} %get-tuple-element.73) | copy-start | bytes 9437188
  425.3 11.0 %slice-start.3 = ((s8[6291456]{0:T(1024)(128)(4,1)}), s8[4194304]{0:T(1024)(128)(4,1)S(1)}, s32[]{:S(2)}) async-start(s8[6291456]{0:T(1024)(128)(4,1)} %bitcast.249), calls=%async_computation.22 | async-start | bytes 8388608
  425.3 11.0 %copy-start.61 = (f32[768]{0:T(1024)S(1)}, f32[768]{0:T(1024)}, u32[]{:S(2)}) copy-start(f32[768]{0:T(1024)} %slice.150) | copy-start | bytes 9220
  461.2 30.9 %all-to-all-start.3 = ((bf16[8,4,32,768]{3,2,1,0:T(8,128)(2,1)}), bf16[8,4,32,768]{3,2,1,0:T(8,128)(2,1)S(1)}, u32[]{:S(2)}, u32[]{:S(2)}) async-start(bf16[8,4,32,768]{3,2,1,0:T(8,128)(2,1)} %bitcast.248), calls=%async_computation.3 | async-start | bytes 3145728 | tf_op jit(solution)/shard_map/all_to_all | solution.py:241
  465.0 166.9 %reduce-scatter.4.cloned.1.call-start = ((), (), s32[]{:S(2)}) async-start(), calls=%async_computation.15 | async-start | bytes 5308416 | tf_op jit(solution)/shard_map/reduce_scatter | solution.py:341
  475.6 16.5 %copy-start.53 = (f32[4,768]{1,0:T(4,128)S(1)}, f32[4,768]{1,0:T(4,128)}, u32[]{:S(2)}) copy-start(f32[4,768]{1,0:T(4,128)} %copy-done.52) | copy-start | bytes 36868
  520.6 7.6 copy-start.23
  563.9 148.1 %reduce-scatter.8.cloned.1.call-start = ((), (), s32[]{:S(2)}) async-start(), calls=%async_computation.17 | async-start | bytes 10616832 | tf_op jit(solution)/shard_map/reduce_scatter | solution.py:341
  579.1 188.3 %all-to-all-start.1 = ((bf16[8,4,32,768]{3,2,1,0:T(8,128)(2,1)}), bf16[8,4,32,768]{3,2,1,0:T(8,128)(2,1)S(1)}, u32[]{:S(2)}, u32[]{:S(2)}) async-start(bf16[8,4,32,768]{3,2,1,0:T(8,128)(2,1)} %bitcast.32), calls=%async_computation.1 | async-start | bytes 3145728 | tf_op jit(solution)/shard_map/all_to_all | solution.py:241
  582.7 183.1 %all-reduce.8.cloned.1.call-start = ((), (), s32[]{:S(2)}) async-start(), calls=%async_computation.14 | async-start | bytes 147456 | tf_op jit(solution)/shard_map/psum | solution.py:297
  591.2 7.6 copy-start.14
  591.2 7.6 copy-start.31
  598.9 113.1 %copy-start.76 = (f32[1,2]{1,0:T(1,128)S(1)}, f32[1,2]{1,0:T(1,128)}, u32[]{:S(2)}) copy-start(f32[1,2]{1,0:T(1,128)} %get-tuple-element.59) | copy-start | bytes 28
  598.9 113.2 %copy-start.72 = (bf16[2,96]{1,0:T(2,128)(2,1)S(1)}, bf16[2,96]{1,0:T(2,128)(2,1)}, u32[]{:S(2)}) copy-start(bf16[2,96]{1,0:T(2,128)(2,1)} %copy-done.71) | copy-start | bytes 1156
  598.9 113.2 %copy-start.74 = (pred[2]{0:T(512)(128)(4,1)S(1)}, pred[2]{0:T(512)(128)(4,1)}, u32[]{:S(2)}) copy-start(pred[2]{0:T(512)(128)(4,1)} %copy-done.73) | copy-start | bytes 10
  602.7 263.3 %all-reduce.10.cloned.1.call-start = ((), (), s32[]{:S(2)}) async-start(), calls=%async_computation.18 | async-start | bytes 4718592 | tf_op jit(solution)/shard_map/psum | solution.py:342
  781.5 87.3 %copy-start.78 = (f32[480]{0:T(512)}, f32[480]{0:T(512)S(1)}, u32[]{:S(2)}) copy-start(f32[480]{0:T(512)S(1)} %get-tuple-element.32) | copy-start | bytes 5764
  (51 other events, 171.9 us)
Sparse Core Ops, SparseCore 0:
  15.8 53.8 all-reduce.5
  71.6 35.0 all-gather.8
  108.6 23.9 all-gather.10
  134.3 43.2 all-gather.12
  179.3 26.1 all-gather.14
  207.3 38.7 all-gather.16
  248.0 38.7 all-gather.18
  425.4 62.8 reduce-scatter.5
  564.0 67.7 reduce-scatter.3
  635.2 76.7 reduce-scatter.7
  715.6 50.1 all-reduce.7
  768.2 97.7 all-reduce.9
where the time goes:
time: 898 us; the launch traced here: 886 us
  waiting for transfers between devices  321 us (36%)
  matrix products  218 us (24%)
  local copies, waits for them, and re-layouts  173 us (19%)
  other arithmetic  103 us (11%)
  blocking collectives  37.5 us (4%)
  starting transfers between devices  16.7 us (2%)
  between operations  15.7 us (2%)
    reduce_scatter x3, waiting for transfers between devices, total(): lax.psum_scatter(packed, 'shard', scatter_dimension=0, tiled=True)[0]  109 us
    psum x1, waiting for transfers between devices, total(): share = lax.psum(share, 'grp').astype(jnp.float32)  64 us
    psum x1, waiting for transfers between devices, body(): small_grads = lax.psum(small_grads, 'shard')  42.7 us
    all_gather x1, waiting for transfers between devices, body(): space_qkv_full = lax.all_gather(space_qkv, 'shard', axis=0, tiled=True)  35.3 us
    psum x1, waiting for transfers between devices, body(): small = lax.psum(small, 'shard')  35.1 us
    convert_element_type x1, other arithmetic, feed_forward(): active = jax.nn.gelu(upward, approximate=False).astype(jnp.bfloat16)  29.8 us
    unnamed x176, local copies, waits for them, and re-layouts  23.9 us
    all_to_all x2, waiting for transfers between devices, to_columns(): lax.all_to_all(parts, 'shard', split_axis=0, concat_axis=0, tiled=True)  23 us
  transfers between devices with their start and end apart: 16, of which 8 were waited for; matrix products, arithmetic and copies ran while one was open for 37% of the time, Pallas kernels for 0%

commit v1 on v0

--- a/solution.py
+++ b/solution.py
@@ -3,6 +3,7 @@
 import jax.numpy as jnp
 from jax import lax
 from jax.sharding import PartitionSpec as P
+from jax.lax import axis_size, ppermute
 
 HEADS = 12
 HEAD_DIM = 64
@@ -294,7 +295,12 @@
     )
     mod_part = jnp.concatenate(space_mods + time_mods + mlp_mods, axis=1)
     small_grads = jnp.concatenate([mod_part.reshape(-1), grad_up_bias, grad_down_bias])
-    small_grads = lax.psum(small_grads, "shard")
+    n_dev_all = axis_size("shard")
+    raw_out = small_grads
+    for m in [[(it, it ^ s) for it in range(n_dev_all)] for s in (1, 2, 4, 8, 16) if s < n_dev_all]:
+        known = ppermute(raw_out, axis_name="shard", perm=m)
+        raw_out = raw_out + known
+    small_grads = raw_out
     mod_size = clips * 9 * width
     grad_modul = small_grads[:mod_size].reshape(clips, 9 * width).astype(jnp.bfloat16)
     up_dev = up_bias.shape[0]

time: 898 us -> 843 us (0.939)
  waiting for transfers between devices: 321 us -> 269 us
    psum x1 -> x0, waiting for transfers between devices: 42.7 us -> none  [body(): small_grads = lax.psum(small_grads, 'shard')]
    psum x1, waiting for transfers between devices: 64 us -> 51.1 us  [total(): share = lax.psum(share, 'grp').astype(jnp.float32)]
  transfers between devices with their start and end apart: 16 -> 18, of which waited for: 8 -> 8; matrix products, arithmetic and copies ran while one was open for 37% -> 40% of each run, Pallas kernels for 0% -> 0%
where the time goes in v1:
time: 843 us; the launch traced here: 831 us
  waiting for transfers between devices  269 us (32%)
  matrix products  218 us (26%)
  local copies, waits for them, and re-layouts  171 us (20%)
  other arithmetic  103 us (12%)
  blocking collectives  34.7 us (4%)
  starting transfers between devices  20.2 us (2%)
  between operations  15.4 us (2%)
    reduce_scatter x3, waiting for transfers between devices, total(): lax.psum_scatter(packed, 'shard', scatter_dimension=0, tiled=True)[0]  110 us
    psum x1, waiting for transfers between devices, total(): share = lax.psum(share, 'grp').astype(jnp.float32)  51.1 us
    all_gather x1, waiting for transfers between devices, body(): space_qkv_full = lax.all_gather(space_qkv, 'shard', axis=0, tiled=True)  35.3 us
    psum x1, waiting for transfers between devices, body(): small = lax.psum(small, 'shard')  35 us
    convert_element_type x1, other arithmetic, feed_forward(): active = jax.nn.gelu(upward, approximate=False).astype(jnp.bfloat16)  29.8 us
    unnamed x176, local copies, waits for them, and re-layouts  24 us
    all_to_all x2, waiting for transfers between devices, to_columns(): lax.all_to_all(parts, 'shard', split_axis=0, concat_axis=0, tiled=True)  23 us
    reshape x3, local copies, waits for them, and re-layouts, total(): part.astype(jnp.bfloat16).reshape(shards, -1, width)  22 us
  transfers between devices with their start and end apart: 18, of which 8 were waited for; matrix products, arithmetic and copies ran while one was open for 40% of the time, Pallas kernels for 0%

profile of v1, /device:TPU:0, one launch (start us, length us, event | category | flops | bytes accessed | tf_op | source)
XLA Modules:
  0.0 831.3 jit_solution(3027769625904227659)
XLA Ops:
  24.4 5.2 all-to-all-start.2
  34.7 35.0 %all-reduce.5.cloned.1.call-done = f32[17664]{0:T(1024)} async-done(((f32[17664]{0:T(1024)}), f32[17664]{0:T(1024)}) %all-reduce.5.cloned.1.call-update) | async-done | bytes 70672 | tf_op jit(solution)/shard_map/psum | solution.py:205
  71.3 35.3 %all-gather.9.cloned.1.call-done = bf16[768,2304]{1,0:T(8,128)(2,1)} async-done(((bf16[96,2304]{1,0:T(8,128)(2,1)}), bf16[768,2304]{1,0:T(8,128)(2,1)}) %all-gather.9.cloned.1.call-update) | async-done | bytes 3538960 | tf_op jit(solution)/shard_map/all_gather | solution.py:186
  106.7 7.0 fusion.9
  129.4 8.7 %convolution_convert_fusion.3 = bf16[4,12,64,256]{3,2,1,0:T(8,128)(2,1)} fusion(bf16[4,256,12,64]{1,3,2,0:T(8,128)(2,1)S(1)} %bitcast.236, f32[4,12,256,256]{2,3,1,0:T(8,128)} %copy-done.3, f32[4,12,256]{2,1,0:T(8,128)S(1)} %log_add_fusion.1), kind=kOutput, calls=%fused_computation.132 | convolution fusion | flops 412876800 | bytes 15777792 | tf_op jit(solution)/shard_map/bmhlk,bkmhe->blmhe/dot_general | solution.py:45
  138.1 5.9 add_convert_fusion.3
  156.1 23.0 %all-to-all-done = bf16[8,4,32,768]{3,2,1,0:T(8,128)(2,1)S(1)} async-done(((bf16[8,4,32,768]{3,2,1,0:T(8,128)(2,1)}), bf16[8,4,32,768]{3,2,1,0:T(8,128)(2,1)S(1)}, u32[]{:S(2)}, u32[]{:S(2)}) %all-to-all-start) | async-done | bytes 1572896 | tf_op jit(solution)/shard_map/all_to_all | solution.py:237
  182.4 5.2 select_convert_fusion.2
  189.8 7.0 convolution_convert_fusion
  199.2 6.1 reshape.639
  205.3 5.9 reshape.640
  211.1 6.0 reshape.638
  217.1 8.0 multiply_reduce_fusion.3
  238.5 6.5 convert_element_type.258
  245.0 5.8 multiply_add_fusion.3
  255.4 11.6 %fusion.8 = (u16[2,32,3072]{2,1,0:T(8,128)(2,1)S(1)}, u16[2,32,3072]{2,1,0:T(8,128)(2,1)S(1)}, f32[2,16,32,3072]{3,2,1,0:T(8,128)S(1)}) fusion(f32[3072]{0:T(1024)S(1)} %slice.149, bf16[768,3072]{1,0:T(8,128)(2,1)} %all-gather.17.cloned.1.call-done, f32[2,16,32,768]{3,2,1,0:T(8,128)} %get-tuple-element.73, f32[2,768]{1,0:T(2,128)S(1)} %get-tuple-element.54, ...), kind=kOutput, calls=%fused_computation.51 | convolution fusion | flops 4879417344 | bytes 21266432 | tf_op jit(solution)/shard_map/blmd,df->blmf/dot_general | solution.py:118
  272.0 29.8 %multiply_convert_fusion.1 = (bf16[2,16,32,3072]{3,2,1,0:T(8,128)(2,1)}, f32[2,16,32,3072]{3,2,1,0:T(8,128)}) fusion(f32[2,16,32,3072]{3,2,1,0:T(8,128)S(1)} %get-tuple-element.75, f32[3072]{0:T(1024)S(1)} %slice.149, u16[2,32,3072]{2,1,0:T(8,128)(2,1)S(1)} %get-tuple-element.16, u16[2,32,3072]{2,1,0:T(8,128)(2,1)S(1)} %get-tuple-element.15), kind=kLoop, calls=%fused_computation.21 | loop fusion | flops 223346688 | bytes 32256000 | tf_op jit(solution)/shard_map/convert_element_type | solution.py:121
  301.8 19.6 %convert_reduce_fusion = (f32[3072]{0:T(1024)}, bf16[2,16,32,3072]{3,2,1,0:T(8,128)(2,1)}) fusion(f32[2,16,32,3072]{3,2,1,0:T(8,128)} %get-tuple-element.37, bf16[3072,768]{1,0:T(8,128)(2,1)} %all-gather.19.cloned.1.call-done, f32[2,16,32,768]{3,2,1,0:T(8,128)} %bitcast.240, f32[2,768]{1,0:T(2,128)S(1)} %get-tuple-element.55, ...), kind=kOutput, calls=%fused_computation.17 | convolution fusion | flops 4886885376 | bytes 39352320 | tf_op jit(solution)/shard_map/blmd,fd->blmf/dot_general | solution.py:136
  321.5 9.9 %multiply_reduce_fusion.5 = (f32[2,768]{1,0:T(2,128)}, f32[2,16,32]{2,1,0:T(8,128)S(1)}, f32[2,16,32]{2,1,0:T(8,128)S(1)}, f32[2,768]{1,0:T(2,128)}, f32[2,16,32,768]{3,2,1,0:T(8,128)S(1)}) fusion(f32[2,16,32,768]{3,2,1,0:T(8,128)S(1)} %copy-done.10, f32[2,16,32]{2,1,0:T(8,128)S(1)} %add_rsqrt_fusion, f32[2,16,32]{2,1,0:T(8,128)S(1)} %broadcast_multiply_fusion.4, ...), kind=kOutput, calls=%fused_computation.88 | convolution fusion | flops 4838910976 | bytes 17336320 | tf_op jit(solution)/shard_map/blmf,df->blmd/dot_general | solution.py:143
  338.0 6.2 reshape.645
  344.2 13.1 %multiply_reduce_fusion.2 = (f32[2,32,12,16]{3,2,1,0:T(8,128)S(1)}, f32[2,32,12,16,16]{3,4,2,1,0:T(8,128)}) fusion(f32[2,32,12,16,16]{3,4,2,1,0:T(8,128)} %copy-done.5, f32[2,32,12,16]{3,2,1,0:T(8,128)} %copy-done.28, bf16[2,16,32,12,64]{4,3,2,1,0:T(8,128)(2,1)} %reshape.638, bf16[2,16,32,12,64]{4,3,2,1,0:T(8,128)(2,1)} %reshape.645), kind=kOutput, calls=%fused_computation.47 | convolution fusion | flops 25939968 | bytes 4816896 | tf_op jit(solution)/shard_map/blmhe,bkmhe->bmhlk/dot_general | solution.py:58
  357.4 6.7 convert_bitcast_fusion.1
  376.4 5.2 reshape.646
  381.7 5.1 copy.175
  386.7 6.1 reshape.647
  397.8 6.1 reshape.648
  408.2 5.8 bitcast_convert_fusion.2
  414.1 6.8 reshape.657
  425.5 10.9 %multiply_reduce_fusion.7 = (f32[2,768]{1,0:T(2,128)}, f32[2,16,32]{2,1,0:T(8,128)S(1)}, f32[2,16,32]{2,1,0:T(8,128)S(1)}, f32[2,768]{1,0:T(2,128)}, f32[2,16,32,768]{3,2,1,0:T(8,128)}) fusion(f32[2,16,32,768]{3,2,1,0:T(8,128)} %bitcast.258, f32[2,16,32]{2,1,0:T(8,128)S(1)} %bitcast.274, f32[2,16,32]{2,1,0:T(8,128)S(1)} %bitcast.270, ...), kind=kOutput, calls=%fused_computation.90 | convolution fusion | flops 3630951424 | bytes 14583808 | tf_op jit(solution)/shard_map/blme,de->blmd/dot_general | solution.py:106
  436.4 9.4 %multiply_add_fusion.2 = (bf16[2,16,32,768]{3,2,1,0:T(8,128)(2,1)}, f32[2,16,32,768]{3,2,1,0:T(8,128)}) fusion(f32[2,16,32,768]{3,2,1,0:T(8,128)S(1)} %copy-done.11, f32[768]{0:T(1024)S(1)} %copy-done.62, f32[2,768]{1,0:T(2,128)S(1)} %get-tuple-element.55, bf16[2,16,32,3072]{3,2,1,0:T(8,128)(2,1)S(1)} %bitcast.250, ...), kind=kOutput, calls=%fused_computation.103 | convolution fusion | flops 4834983936 | bytes 18883584 | tf_op jit(solution)/shard_map/blmf,fd->blmd/dot_general | solution.py:122
  465.1 10.6 %bitcast_convert_fusion.1 = bf16[768,3072]{1,0:T(8,128)(2,1)} fusion(bf16[2,16,32,3072]{3,2,1,0:T(8,128)(2,1)} %get-tuple-element.86, f32[2,16,32,768]{3,2,1,0:T(8,128)} %get-tuple-element.73, f32[2,768]{1,0:T(2,128)S(1)} %copy-done.66, f32[2,768]{1,0:T(2,128)S(1)} %get-tuple-element.53, f32[2,16,32]{2,1,0:T(8,128)S(1)} %add_rsqrt_fusion, ...), kind=kOutput, calls=%fused_computation.39 | convolution fusion | flops 4838129664 | bytes 14176256 | tf_op jit(solution)/shard_map/blmd,blmf->df/dot_general | solution.py:141
  475.7 8.5 %reshape.660 = bf16[8,384,768]{2,1,0:T(8,128)(2,1)} reshape(bf16[768,3072]{1,0:T(8,128)(2,1)} %bitcast_convert_fusion.1) | data formatting | bytes 9437184 | tf_op jit(solution)/shard_map/reshape | solution.py:344
  484.2 8.1 all-to-all-done.3
  503.0 8.1 convolution_convert_fusion.2
  513.8 6.9 multiply_reduce_fusion
  520.8 7.6 multiply_convert_fusion
  534.3 6.0 multiply_convert_fusion.6
  543.0 8.8 %bitcast_convert_fusion.3 = bf16[768,2304]{1,0:T(8,128)(2,1)} fusion(bf16[4,256,768]{2,1,0:T(8,128)(2,1)S(1)} %copy-done.45, bf16[4,256,768]{2,1,0:T(8,128)(2,1)} %copy.184, bf16[4,256,768]{2,1,0:T(8,128)(2,1)} %copy.183, f32[4,256,768]{2,1,0:T(8,128)} %param.21, f32[4,768]{1,0:T(4,128)S(1)} %copy-done.64, f32[4,768]{1,0:T(4,128)S(1)} %copy-done.55, ...), kind=kOutput, calls=%fused_computation.43 | convolution fusion | flops 3643736064 | bytes 11436032 | tf_op jit(solution)/shard_map/blmd,blme->de/dot_general | solution.py:105
  551.8 6.7 reshape.654
  564.0 8.2 bitcast_convert_fusion
  572.3 6.8 pad_maximum_fusion
  591.3 7.0 multiply_reduce_fusion.8
  602.5 29.5 %reduce-scatter.4.cloned.1.call-done = bf16[1,384,768]{2,1,0:T(8,128)(2,1)} async-done(((bf16[8,384,768]{2,1,0:T(8,128)(2,1)}), bf16[1,384,768]{2,1,0:T(8,128)(2,1)}) %reduce-scatter.4.cloned.1.call-update) | async-done | bytes 589840 | tf_op jit(solution)/shard_map/reduce_scatter | solution.py:347
  631.9 80.2 %reduce-scatter.8.cloned.1.call-done = bf16[1,768,768]{2,1,0:T(8,128)(2,1)} async-done(((bf16[8,768,768]{2,1,0:T(8,128)(2,1)}), bf16[1,768,768]{2,1,0:T(8,128)(2,1)}) %reduce-scatter.8.cloned.1.call-update) | async-done | bytes 1179664 | tf_op jit(solution)/shard_map/reduce_scatter | solution.py:347
  718.4 11.4 %all-gather.1 = bf16[4,2,96]{2,1,0:T(2,128)(2,1)S(1)} all-gather(bf16[1,2,96]{2,1,0:T(2,128)(2,1)S(1)} %fusion.91), channel_id=1, replica_groups=mesh['grp'=4,'shard'=8] {'grp'}, dimensions={0}, use_global_device_ids=true | all-gather | bytes 1920 | tf_op jit(solution)/shard_map/all_gather | solution.py:321
  731.9 8.9 %all-reduce = (f32[8]{0:T(128)S(1)}, f32[480]{0:T(512)S(1)}) all-reduce(f32[8]{0:T(128)S(1)} %reshape.652, f32[480]{0:T(512)S(1)} %pad_maximum_fusion.8), channel_id=1, replica_groups=mesh['grp'=4,'shard'=8] {'grp'}, use_global_device_ids=true, to_apply=%region_20.23 | all-reduce | flops 488 | bytes 3904 | tf_op jit(solution)/shard_map/psum | solution.py:328
  741.4 14.4 %all-gather = bf16[4,2,6912]{2,1,0:T(2,128)(2,1)S(1)} all-gather(bf16[1,2,6912]{2,1,0:T(2,128)(2,1)S(1)} %reshape.753), channel_id=1, replica_groups=mesh['grp'=4,'shard'=8] {'grp'}, dimensions={0}, use_global_device_ids=true | all-gather | bytes 138240 | tf_op jit(solution)/shard_map/all_gather | solution.py:309
  760.4 51.1 %all-reduce.7.cloned.1.call-done = (bf16[384,768]{1,0:T(8,128)(2,1)}, bf16[384,768]{1,0:T(8,128)(2,1)}, bf16[768,768]{1,0:T(8,128)(2,1)}) async-done(((bf16[384,768]{1,0:T(8,128)(2,1)}, bf16[384,768]{1,0:T(8,128)(2,1)}, bf16[768,768]{1,0:T(8,128)(2,1)}), (bf16[384,768]{1,0:T(8,128)(2,1)}, bf16[384,768]{1,0:T(8,128)(2,1)}, bf16[768,768]{1,0:T(8,128)(2,1)})) %all-reduce.7.cloned.1.call-update) | async-done | bytes 2359312 | tf_op jit(solution)/shard_map/psum | solution.py:348
  (360 shorter events, 204.2 us)
Async XLA Ops:
  7.2 11.8 %copy-start.2 = (s32[1,32]{1,0:T(1,128)S(1)}, s32[1,32]{1,0:T(1,128)}, u32[]{:S(2)}) copy-start(s32[1,32]{1,0:T(1,128)} %param.37) | copy-start | bytes 388
  7.2 12.4 %copy-start.4 = (s32[2,16]{1,0:T(2,128)S(1)}, s32[2,16]{1,0:T(2,128)}, u32[]{:S(2)}) copy-start(s32[2,16]{1,0:T(2,128)} %param.35) | copy-start | bytes 388
  7.2 13.1 %copy-start.1 = (f32[2]{0:T(128)S(1)}, f32[2]{0:T(128)}, u32[]{:S(2)}) copy-start(f32[2]{0:T(128)} %param.36) | copy-start | bytes 28
  7.2 62.5 %all-reduce.5.cloned.1.call-start = ((), (), s32[]{:S(2)}) async-start(), calls=%async_computation.7 | async-start | bytes 147456 | tf_op jit(solution)/shard_map/psum | solution.py:205
  8.0 15.1 %copy-start.73 = (pred[2]{0:T(512)(128)(4,1)}, pred[2]{0:T(512)(128)(4,1)S(1)}, u32[]{:S(2)}) copy-start(pred[2]{0:T(512)(128)(4,1)S(1)} %compare_and_fusion.2) | copy-start | bytes 10
  14.6 8.6 %copy-start.71 = (bf16[2,96]{1,0:T(2,128)(2,1)}, bf16[2,96]{1,0:T(2,128)(2,1)S(1)}, u32[]{:S(2)}) copy-start(bf16[2,96]{1,0:T(2,128)(2,1)S(1)} %gather_fusion.1) | copy-start | bytes 1156
  15.7 91.0 %all-gather.9.cloned.1.call-start = ((), (), s32[]{:S(2)}) async-start(), calls=%async_computation.8 | async-start | bytes 3981312 | tf_op jit(solution)/shard_map/all_gather | solution.py:186
  16.5 121.6 %all-gather.11.cloned.1.call-start = ((), (), s32[]{:S(2)}) async-start(), calls=%async_computation.9 | async-start | bytes 1327104 | tf_op jit(solution)/shard_map/all_gather | solution.py:187
  17.2 172.6 %all-gather.13.cloned.1.call-start = ((), (), s32[]{:S(2)}) async-start(), calls=%async_computation.10 | async-start | bytes 3981312 | tf_op jit(solution)/shard_map/all_gather | solution.py:188
  17.8 227.2 %all-gather.15.cloned.1.call-start = ((), (), s32[]{:S(2)}) async-start(), calls=%async_computation.11 | async-start | bytes 1327104 | tf_op jit(solution)/shard_map/all_gather | solution.py:189
  18.4 237.0 %all-gather.17.cloned.1.call-start = ((), (), s32[]{:S(2)}) async-start(), calls=%async_computation.12 | async-start | bytes 5308416 | tf_op jit(solution)/shard_map/all_gather | solution.py:190
  24.4 120.8 %all-to-all-start.2 = ((bf16[8,4,32,768]{3,2,1,0:T(8,128)(2,1)}), bf16[8,4,32,768]{3,2,1,0:T(8,128)(2,1)}, u32[]{:S(2)}, u32[]{:S(2)}) async-start(bf16[8,4,32,768]{3,2,1,0:T(8,128)(2,1)} %copy.168), calls=%async_computation.2 | async-start | bytes 3145728 | tf_op jit(solution)/shard_map/all_to_all | solution.py:237
  32.3 81.4 %copy-start.58 = (f32[4,256]{1,0:T(4,128)}, f32[4,256]{1,0:T(4,128)S(1)}, u32[]{:S(2)}) copy-start(f32[4,256]{1,0:T(4,128)S(1)} %broadcast_multiply_fusion.8) | copy-start | bytes 12292
  34.7 79.0 %copy-start.60 = (f32[4,256]{1,0:T(4,128)}, f32[4,256]{1,0:T(4,128)S(1)}, u32[]{:S(2)}) copy-start(f32[4,256]{1,0:T(4,128)S(1)} %add_rsqrt_fusion.2) | copy-start | bytes 12292
  71.3 42.4 %copy-start.54 = (f32[4,768]{1,0:T(4,128)}, f32[4,768]{1,0:T(4,128)S(1)}, u32[]{:S(2)}) copy-start(f32[4,768]{1,0:T(4,128)S(1)} %get-tuple-element.52) | copy-start | bytes 36868
  71.3 42.4 %copy-start.63 = (f32[4,768]{1,0:T(4,128)}, f32[4,768]{1,0:T(4,128)S(1)}, u32[]{:S(2)}) copy-start(f32[4,768]{1,0:T(4,128)S(1)} %get-tuple-element.51) | copy-start | bytes 36868
  71.3 66.7 %copy-start.52 = (f32[4,768]{1,0:T(4,128)}, f32[4,768]{1,0:T(4,128)S(1)}, u32[]{:S(2)}) copy-start(f32[4,768]{1,0:T(4,128)S(1)} %get-tuple-element.50) | copy-start | bytes 36868
  127.4 10.6 %copy-start.43 = (f32[4,12,256]{2,1,0:T(8,128)}, f32[4,12,256]{2,1,0:T(8,128)S(1)}, u32[]{:S(2)}) copy-start(f32[4,12,256]{2,1,0:T(8,128)S(1)} %log_add_fusion.1) | copy-start | bytes 147460
  129.4 8.7 %copy-start.25 = (bf16[4,256,1,768]{1,3,0,2:T(8,128)(2,1)}, bf16[4,256,1,768]{1,3,0,2:T(8,128)(2,1)S(1)}, u32[]{:S(2)}) copy-start(bf16[4,256,1,768]{1,3,0,2:T(8,128)(2,1)S(1)} %copy.156) | copy-start | bytes 4718596
  145.2 34.0 %all-to-all-start = ((bf16[8,4,32,768]{3,2,1,0:T(8,128)(2,1)}), bf16[8,4,32,768]{3,2,1,0:T(8,128)(2,1)S(1)}, u32[]{:S(2)}, u32[]{:S(2)}) async-start(bf16[8,4,32,768]{3,2,1,0:T(8,128)(2,1)} %bitcast.226), calls=%async_computation | async-start | bytes 3145728 | tf_op jit(solution)/shard_map/all_to_all | solution.py:237
  148.8 153.0 %all-gather.19.cloned.1.call-start = ((), (), s32[]{:S(2)}) async-start(), calls=%async_computation.13 | async-start | bytes 5308416 | tf_op jit(solution)/shard_map/all_gather | solution.py:191
  149.5 452.9 %reduce-scatter.6.cloned.1.call-start = ((), (), s32[]{:S(2)}) async-start(), calls=%async_computation.15 | async-start | bytes 5308416 | tf_op jit(solution)/shard_map/reduce_scatter | solution.py:347
  152.9 102.5 %copy-start.65 = (f32[2,768]{1,0:T(2,128)}, f32[2,768]{1,0:T(2,128)S(1)}, u32[]{:S(2)}) copy-start(f32[2,768]{1,0:T(2,128)S(1)} %get-tuple-element.54) | copy-start | bytes 18436
  182.4 62.6 %copy-start.6 = (bf16[32,32,768]{2,1,0:T(8,128)(2,1)}, bf16[32,32,768]{2,1,0:T(8,128)(2,1)S(1)}, u32[]{:S(2)}) copy-start(bf16[32,32,768]{2,1,0:T(8,128)(2,1)S(1)} %gather_fusion.5) | copy-start | bytes 4718596
  301.8 19.7 %copy-start.10 = (f32[2,16,32,768]{3,2,1,0:T(8,128)S(1)}, f32[2,16,32,768]{3,2,1,0:T(8,128)}, u32[]{:S(2)}) copy-start(f32[2,16,32,768]{3,2,1,0:T(8,128)} %get-tuple-element.73) | copy-start | bytes 9437188
  321.5 10.0 %copy-start.20 = (bf16[32,32,768]{2,1,0:T(8,128)(2,1)S(1)}, bf16[32,32,768]{2,1,0:T(8,128)(2,1)}, u32[]{:S(2)}) copy-start(bf16[32,32,768]{2,1,0:T(8,128)(2,1)} %gather_fusion.7) | copy-start | bytes 4718596
  338.0 19.4 %slice-start = ((s8[6291456]{0:T(1024)(128)(4,1)}), s8[2097152]{0:T(1024)(128)(4,1)S(1)}, s32[]{:S(2)}) async-start(s8[6291456]{0:T(1024)(128)(4,1)} %bitcast.230), calls=%async_computation.18 | async-start | bytes 4194304
  344.2 13.1 %slice-start.1 = ((s8[6291456]{0:T(1024)(128)(4,1)}), s8[4194304]{0:T(1024)(128)(4,1)S(1)}, s32[]{:S(2)}) async-start(s8[6291456]{0:T(1024)(128)(4,1)} %bitcast.230), calls=%async_computation.19 | async-start | bytes 8388608
  344.2 13.1 %copy-start.29 = (f32[2,32,12,16]{3,2,1,0:T(8,128)S(1)}, f32[2,32,12,16]{3,2,1,0:T(8,128)}, u32[]{:S(2)}) copy-start(f32[2,32,12,16]{3,2,1,0:T(8,128)} %copy-done.28) | copy-start | bytes 147460
  425.4 11.0 %slice-start.2 = ((s8[6291456]{0:T(1024)(128)(4,1)}), s8[2097152]{0:T(1024)(128)(4,1)S(1)}, s32[]{:S(2)}) async-start(s8[6291456]{0:T(1024)(128)(4,1)} %bitcast.249), calls=%async_computation.20 | async-start | bytes 4194304
  425.4 11.0 %copy-start.11 = (f32[2,16,32,768]{3,2,1,0:T(8,128)S(1)}, f32[2,16,32,768]{3,2,1,0:T(8,128)}, u32[]{:S(2)}) copy-start(f32[2,16,32,768]{3,2,1,0:T(8,128)} %get-tuple-element.73) | copy-start | bytes 9437188
  425.4 11.0 %slice-start.3 = ((s8[6291456]{0:T(1024)(128)(4,1)}), s8[4194304]{0:T(1024)(128)(4,1)S(1)}, s32[]{:S(2)}) async-start(s8[6291456]{0:T(1024)(128)(4,1)} %bitcast.249), calls=%async_computation.21 | async-start | bytes 8388608
  425.4 11.0 %copy-start.62 = (f32[768]{0:T(1024)S(1)}, f32[768]{0:T(1024)}, u32[]{:S(2)}) copy-start(f32[768]{0:T(1024)} %slice.150) | copy-start | bytes 9220
  461.3 30.9 %all-to-all-start.3 = ((bf16[8,4,32,768]{3,2,1,0:T(8,128)(2,1)}), bf16[8,4,32,768]{3,2,1,0:T(8,128)(2,1)S(1)}, u32[]{:S(2)}, u32[]{:S(2)}) async-start(bf16[8,4,32,768]{3,2,1,0:T(8,128)(2,1)} %bitcast.248), calls=%async_computation.3 | async-start | bytes 3145728 | tf_op jit(solution)/shard_map/all_to_all | solution.py:242
  465.0 166.9 %reduce-scatter.4.cloned.1.call-start = ((), (), s32[]{:S(2)}) async-start(), calls=%async_computation.14 | async-start | bytes 5308416 | tf_op jit(solution)/shard_map/reduce_scatter | solution.py:347
  475.7 16.5 %copy-start.53 = (f32[4,768]{1,0:T(4,128)S(1)}, f32[4,768]{1,0:T(4,128)}, u32[]{:S(2)}) copy-start(f32[4,768]{1,0:T(4,128)} %copy-done.52) | copy-start | bytes 36868
  520.7 7.6 copy-start.23
  564.0 148.2 %reduce-scatter.8.cloned.1.call-start = ((), (), s32[]{:S(2)}) async-start(), calls=%async_computation.16 | async-start | bytes 10616832 | tf_op jit(solution)/shard_map/reduce_scatter | solution.py:347
  579.1 150.8 %all-to-all-start.1 = ((bf16[8,4,32,768]{3,2,1,0:T(8,128)(2,1)}), bf16[8,4,32,768]{3,2,1,0:T(8,128)(2,1)S(1)}, u32[]{:S(2)}, u32[]{:S(2)}) async-start(bf16[8,4,32,768]{3,2,1,0:T(8,128)(2,1)} %bitcast.32), calls=%async_computation.1 | async-start | bytes 3145728 | tf_op jit(solution)/shard_map/all_to_all | solution.py:242
  582.7 228.8 %all-reduce.7.cloned.1.call-start = ((), (), s32[]{:S(2)}) async-start(), calls=%async_computation.17 | async-start | bytes 4718592 | tf_op jit(solution)/shard_map/psum | solution.py:348
  591.3 7.6 copy-start.31
  601.6 116.6 %copy-start.72 = (bf16[2,96]{1,0:T(2,128)(2,1)S(1)}, bf16[2,96]{1,0:T(2,128)(2,1)}, u32[]{:S(2)}) copy-start(bf16[2,96]{1,0:T(2,128)(2,1)} %copy-done.71) | copy-start | bytes 1156
  601.6 116.6 %copy-start.74 = (pred[2]{0:T(512)(128)(4,1)S(1)}, pred[2]{0:T(512)(128)(4,1)}, u32[]{:S(2)}) copy-start(pred[2]{0:T(512)(128)(4,1)} %copy-done.73) | copy-start | bytes 10
  601.6 116.7 %copy-start.76 = (f32[1,2]{1,0:T(1,128)S(1)}, f32[1,2]{1,0:T(1,128)}, u32[]{:S(2)}) copy-start(f32[1,2]{1,0:T(1,128)} %get-tuple-element.59) | copy-start | bytes 28
  602.0 110.1 %collective-permute-start = (f32[17664]{0:T(1024)S(1)}, f32[17664]{0:T(1024)S(1)}, u32[]{:S(2)}, u32[]{:S(2)}) collective-permute-start(f32[17664]{0:T(1024)S(1)} %pad_maximum_fusion.7), channel_id=1, source_target_pairs={{0,1},{1,0},{2,3},{3,2},{4,5},{5,4},{6,7},{7,6},{8,9},{9,8},{10,11... | collective-permute-start | bytes 211976 | tf_op jit(solution)/shard_map/ppermute | solution.py:301
  712.2 4.4 collective-permute-start.1
  716.6 13.1 %collective-permute-start.2 = (f32[17664]{0:T(1024)S(1)}, f32[17664]{0:T(1024)S(1)}, u32[]{:S(2)}, u32[]{:S(2)}) collective-permute-start(f32[17664]{0:T(1024)S(1)} %add.375), channel_id=1, source_target_pairs={{0,4},{1,5},{2,6},{3,7},{4,0},{5,1},{6,2},{7,3},{8,12},{9,13},{10,... | collective-permute-start | bytes 211976 | tf_op jit(solution)/shard_map/ppermute | solution.py:301
  740.8 73.4 %copy-start.78 = (f32[480]{0:T(512)}, f32[480]{0:T(512)S(1)}, u32[]{:S(2)}) copy-start(f32[480]{0:T(512)S(1)} %get-tuple-element.32) | copy-start | bytes 5764
  (53 other events, 186.9 us)
Sparse Core Ops, SparseCore 0:
  15.8 53.8 all-reduce.4
  71.6 35.0 all-gather.8
  108.6 23.9 all-gather.10
  134.3 43.2 all-gather.12
  179.3 26.2 all-gather.14
  207.3 38.7 all-gather.16
  248.0 38.8 all-gather.18
  425.5 62.8 reduce-scatter.5
  564.1 67.7 reduce-scatter.3
  635.3 76.8 reduce-scatter.7
  714.7 96.7 all-reduce.6
